TPU v7x, 512 devices: a whole 4x4x16 slice. The times are simulated.
512 devices in a mesh: dp: 8 (over y, core), mp: 64 (over x, z).
Axes of the slice: x: 4, y: 4, z: 16, core: 2. Of those that a mesh axis runs over, the one named last changes fastest.
Arguments:
- query: bfloat16 [2048, 4096], P('dp', 'mp'), may hold values from -0.75 to 0.75
- kv_cache: bfloat16 [16384, 8192], P('dp', 'mp'), may hold values from -4 to 4, as said below
- out_grad: bfloat16 [2048, 4096], P('dp', 'mp'), may hold values from -384 to 384
- source_lengths: int32 [8, 8], P('dp'), may hold values from 1 to 512, 2048 in all within a row
- target_lengths: int32 [8, 8], P('dp'), may hold values from 1 to 64, 256 in all within a row
- low_rank: bfloat16 [16384, 32], P(('dp', 'mp')), may hold values from -0.125 to 0.125
- adapter_up_matrix: bfloat16 [32, 4096], replicated, may hold values from -0.09375 to 0.09375
Outputs:
- query_grad: bfloat16 [2048, 4096], P('dp', 'mp')
- key_gradient: bfloat16 [16384, 4096], P(('dp', 'mp'))
- value_grad: bfloat16 [16384, 4096], P(('dp', 'mp'))
- low_rank_gradient: float32 [16384, 32], P(('dp', 'mp'))
- adapter_up_gradient: float32 [4096, 32], P(('dp', 'mp'))
Inputs may be any that keep to these rules, and one draw needn't show every extreme that they name: `source_lengths`: each row sums to 2048; its largest entry is exactly 512. `target_lengths`: each row sums to 256; its largest entry is exactly 64. `kv_cache`: the key columns lie within -0.75 to 0.75.
All inputs are finite; a program needn't handle non-finite values.
Results may differ from a plain program's by a relative error of at most 0.0053.
Values may be sent and summed in bfloat16 or wider, within the bound.
A program may use at most 64 MiB of HBM per device.

v0:
```python
import math

import jax
import jax.numpy as jnp
from jax import lax
from jax.sharding import PartitionSpec as P

HS = 64


adapter_factor = 2.0


def doc_index(lengths, count):
    ends = jnp.cumsum(lengths)
    position = jnp.arange(count, dtype=jnp.int32)
    return jnp.sum((position[:, None] >= ends[None, :]).astype(jnp.int32), axis=1)


def tile_terms(query_rows, grad_rows, key_rows, value_rows, row_doc, col_doc):
    scores = jnp.einsum("qhd,khd->hqk", query_rows, key_rows, preferred_element_type=jnp.float32)
    allowed = (row_doc[:, None] == col_doc[None, :])[None]
    expo = jnp.where(allowed, jnp.exp(scores), jnp.zeros_like(scores))
    dprob = jnp.einsum("qhd,khd->hqk", grad_rows, value_rows, preferred_element_type=jnp.float32)
    return (expo, dprob)


def tile_grads(query_rows, grad_rows, key_rows, expo, dprob, total_rows, delta_rows):
    prob = expo / total_rows[:, :, None]
    prob_low = prob.astype(jnp.bfloat16)
    dscore = (prob * (dprob - delta_rows[:, :, None])).astype(jnp.bfloat16)
    query_part = jnp.einsum("hqk,khd->qhd", dscore, key_rows, preferred_element_type=jnp.float32)
    key_part = jnp.einsum("hqk,qhd->khd", dscore, query_rows, preferred_element_type=jnp.float32)
    value_part = jnp.einsum("hqk,qhd->khd", prob_low, grad_rows, preferred_element_type=jnp.float32)
    return (query_part, key_part, value_part)


def dense_pass(query_heads, grad_heads, key_heads, value_heads, tgt_doc, src_doc, key_block):
    src_count = key_heads.shape[0]
    tgt_count, head_count = (query_heads.shape[0], query_heads.shape[1])
    block_count = src_count // key_block

    def take_keys(index):
        start = index * key_block
        key_rows = lax.dynamic_slice_in_dim(key_heads, start, key_block, 0)
        value_rows = lax.dynamic_slice_in_dim(value_heads, start, key_block, 0)
        col_doc = lax.dynamic_slice_in_dim(src_doc, start, key_block, 0)
        return (start, key_rows, value_rows, col_doc)

    def first(index, carry):
        total, weighted = carry
        start, key_rows, value_rows, col_doc = take_keys(index)
        expo, dprob = tile_terms(query_heads, grad_heads, key_rows, value_rows, tgt_doc, col_doc)
        return (total + jnp.sum(expo, axis=2), weighted + jnp.sum(expo * dprob, axis=2))

    zeros = jnp.zeros((head_count, tgt_count), jnp.float32)
    total, weighted = lax.fori_loop(0, block_count, first, (zeros, zeros))
    delta = weighted / total

    def second(index, carry):
        query_acc, key_out, value_out = carry
        start, key_rows, value_rows, col_doc = take_keys(index)
        expo, dprob = tile_terms(query_heads, grad_heads, key_rows, value_rows, tgt_doc, col_doc)
        query_part, key_part, value_part = tile_grads(
            query_heads, grad_heads, key_rows, expo, dprob, total, delta
        )
        key_out = lax.dynamic_update_slice_in_dim(key_out, key_part.astype(jnp.bfloat16), start, 0)
        value_out = lax.dynamic_update_slice_in_dim(
            value_out, value_part.astype(jnp.bfloat16), start, 0
        )
        return (query_acc + query_part, key_out, value_out)

    start_carry = (
        jnp.zeros(query_heads.shape, jnp.float32),
        jnp.zeros(key_heads.shape, jnp.bfloat16),
        jnp.zeros(key_heads.shape, jnp.bfloat16),
    )
    return lax.fori_loop(0, block_count, second, start_carry)


def local(query, kv_cache, out_grad, source_lengths, target_lengths, low_rank, adapter_up_matrix):
    tgt_count = query.shape[0]
    src_count = kv_cache.shape[0]
    head_count = query.shape[1] // HS
    local_width = head_count * HS
    query_heads = query.reshape(tgt_count, head_count, HS)
    grad_heads = out_grad.reshape(tgt_count, head_count, HS)
    both_heads = kv_cache.reshape(src_count, head_count, 2, HS)
    key_heads = both_heads[:, :, 0, :]
    value_heads = both_heads[:, :, 1, :]
    tgt_doc = doc_index(target_lengths[0], tgt_count)
    src_doc = doc_index(source_lengths[0], src_count)
    key_block = math.gcd(src_count, 512)
    query_acc, key_out, value_out = dense_pass(
        query_heads, grad_heads, key_heads, value_heads, tgt_doc, src_doc, key_block
    )
    query_grad = query_acc.reshape(tgt_count, local_width).astype(jnp.bfloat16)
    stacked = jnp.stack(
        [key_out.reshape(src_count, local_width), value_out.reshape(src_count, local_width)]
    )
    rank = adapter_up_matrix.shape[0] // 2
    up_key = adapter_up_matrix[:rank]
    up_value = adapter_up_matrix[rank:]
    owned = lax.all_to_all(stacked, "mp", split_axis=1, concat_axis=2, tiled=True)
    key_gradient = owned[0]
    value_grad = owned[1]
    low_rank_gradient = adapter_factor * jnp.concatenate(
        [
            jnp.einsum("tc,rc->tr", key_gradient, up_key, preferred_element_type=jnp.float32),
            jnp.einsum("tc,rc->tr", value_grad, up_value, preferred_element_type=jnp.float32),
        ],
        axis=1,
    )
    z_key = low_rank[:, :rank]
    z_value = low_rank[:, rank:]
    key_adapter_term = jnp.einsum(
        "tc,tr->cr", key_gradient, z_key, preferred_element_type=jnp.float32
    )
    value_adapter_term = jnp.einsum(
        "tc,tr->cr", value_grad, z_value, preferred_element_type=jnp.float32
    )
    adapter_up_gradient = lax.psum_scatter(
        adapter_factor * jnp.concatenate([key_adapter_term, value_adapter_term], axis=1),
        ("dp", "mp"),
        scatter_dimension=0,
        tiled=True,
    )
    return (query_grad, key_gradient, value_grad, low_rank_gradient, adapter_up_gradient)


def solution(mesh):
    in_specs = (
        P("dp", "mp"),
        P("dp", "mp"),
        P("dp", "mp"),
        P("dp", None),
        P("dp", None),
        P(("dp", "mp"), None),
        P(),
    )
    out_specs = (
        P("dp", "mp"),
        P(("dp", "mp"), None),
        P(("dp", "mp"), None),
        P(("dp", "mp"), None),
        P(("dp", "mp"), None),
    )
    return jax.shard_map(local, mesh=mesh, in_specs=in_specs, out_specs=out_specs, check_vma=False)
```

profile of v0, /device:TPU:1, one launch (start us, length us, event | category | flops | bytes accessed | tf_op | source)
XLA Modules:
  0.0 542.0 jit_solution(2680622482908075447)
XLA Ops:
  7.2 1.2 copy.44
  8.5 0.6 copy-done.6
  9.5 0.6 copy-done.7
  10.4 3.0 while.34
  10.5 0.3 fusion.77
  11.2 0.3 fusion.77
  11.5 0.3 fusion.78
  12.0 0.3 fusion.77
  12.7 0.3 fusion.77
  13.4 5.1 while.35
  18.5 0.8 copy.45
  19.3 1.5 reshape.190
  20.8 19.1 %all-to-all-start = ((bf16[64,2,2048]{2,1,0:T(2,128)(2,1)}), bf16[64,2,2048]{2,1,0:T(2,128)(2,1)S(1)}, u32[]{:S(2)}, u32[]{:S(2)}) async-start(bf16[64,2,2048]{2,1,0:T(2,128)(2,1)} %reshape.190), calls=%async_computation | async-start | bytes 1048576 | tf_op jit(solution)/shard_map/all_to_all | solution.py:104
  40.0 0.6 convert_bitcast_fusion
  40.6 28.8 %all-to-all-done = bf16[64,2,2048]{2,1,0:T(2,128)(2,1)S(1)} async-done(((bf16[64,2,2048]{2,1,0:T(2,128)(2,1)}), bf16[64,2,2048]{2,1,0:T(2,128)(2,1)S(1)}, u32[]{:S(2)}, u32[]{:S(2)}) %all-to-all-start) | async-done | bytes 524320 | tf_op jit(solution)/shard_map/all_to_all | solution.py:104
  69.5 0.7 reshape.191
  70.6 0.5 squeeze.17
  71.3 0.5 squeeze.16
  72.5 0.8 maximum_multiply_fusion
  73.4 0.9 copy-done.4
  74.7 0.7 copy.49
  75.4 458.3 %all-reduce.3.cloned.1.call-done = f32[4096,32]{0,1:T(8,128)} async-done(((f32[4096,32]{0,1:T(8,128)}), f32[4096,32]{0,1:T(8,128)}) %all-reduce.3.cloned.1.call-update) | async-done | bytes 524304
  533.7 0.8 constant_dynamic-slice_fusion
  534.5 0.7 copy.50
  (71 shorter events, 8.6 us)
Async XLA Ops:
  8.4 1.9 copy-start
  8.5 1.9 copy-start.3
  8.5 0.7 copy-start.6
  9.5 0.7 copy-start.7
  20.8 48.6 %all-to-all-start = ((bf16[64,2,2048]{2,1,0:T(2,128)(2,1)}), bf16[64,2,2048]{2,1,0:T(2,128)(2,1)S(1)}, u32[]{:S(2)}, u32[]{:S(2)}) async-start(bf16[64,2,2048]{2,1,0:T(2,128)(2,1)} %reshape.190), calls=%async_computation | async-start | bytes 1048576 | tf_op jit(solution)/shard_map/all_to_all | solution.py:104
  40.0 493.8 %all-reduce.3.cloned.1.call-start = ((), (), s32[]{:S(2)}) async-start(), calls=%async_computation.1 | async-start | bytes 1048576
  71.0 2.3 copy-start.1
  71.3 0.7 copy-start.5
  72.0 2.5 copy-start.2
  73.3 0.9 copy-start.4
Sparse Core Ops, SparseCore 0:
  73.5 460.1 all-reduce.2
where the time goes:
time: 543 us; the launch traced here: 542 us
  waiting for transfers between devices  487 us (90%)
  starting transfers between devices  19.1 us (4%)
  between operations  14.3 us (3%)
  local copies, waits for them, and re-layouts  11.1 us (2%)
  matrix products  7.89 us (1%)
    unnamed x2, waiting for transfers between devices  458 us
    all_to_all x1, waiting for transfers between devices, local(): lax.all_to_all(stacked, 'mp', split_axis=1, concat_axis=2, tiled=True)  28.8 us
    all_to_all x1, starting transfers between devices, local(): lax.all_to_all(stacked, 'mp', split_axis=1, concat_axis=2, tiled=True)  19.1 us
  transfers between devices with their start and end apart: 2, of which 2 were waited for; matrix products, arithmetic and copies ran while one was open for 0% of the time, Pallas kernels for 0%

commit v1 on v0

v1 whole, which is shorter than its diff:
```python
import functools

import jax
import jax.numpy as jnp
from jax import lax
from jax.experimental import pallas as pl
from jax.experimental.pallas import tpu as pltpu
from jax.sharding import PartitionSpec as P

HS = 64
XS, ZS = 4, 16
MP = XS * ZS
DP = 8
NDOC = 8
TQ = 256
S = 2048
OWN = S // MP
RANK2 = 32
ROWS = 256
ADAPTER_FACTOR = 2.0
MESH = pl.DeviceIdType.MESH
F32 = jnp.float32
BF16 = jnp.bfloat16
NT = (((1,), (1,)), ((), ()))
TN = (((0,), (0,)), ((), ()))


def fold8(x):
    return jnp.sum(x.reshape(x.shape[0] // 8, 8, x.shape[1]), axis=0)


def far_first(u):
    half = (u + 1) // 2
    return jnp.where(u % 2 == 1, 8 - half, 8 + half) % ZS


def exchange_kernel(
    q_hbm, kv_hbm, g_hbm, slen, tlen, lr_hbm,
    recv, adapter_recv, qg_out,
    q_v, kv_v, g_v, lr_v, w1, expo_s, dprob_s, ds_s, msg, lr_all, lr_full, adapter_send,
    in_sem, send_sem, recv_sem, lrz_send, lrz_recv, lrx_send, lrx_recv, ad_send, ad_recv, own_sem,
):
    p = lax.axis_index("dp")
    m = lax.axis_index("mp")
    x = m // ZS
    z = m % ZS
    ga = m // 8
    gb = m % 8
    self_adapter = jnp.logical_and(p == ga, gb == ga)

    barrier = pltpu.get_barrier_semaphore()

    def greet(s, _):
        pl.semaphore_signal(barrier, inc=1, device_id=(p, (m + s) % MP), device_id_type=MESH)
        return 0

    lax.fori_loop(1, MP, greet, 0)
    src_head = 8 * p + m // 8
    for j in range(DP):
        not_me = jnp.logical_not(jnp.logical_and(p == j, src_head == m))

        @pl.when(not_me)
        def _():
            pl.semaphore_signal(barrier, inc=1, device_id=(j, src_head), device_id_type=MESH)

    loads = [
        pltpu.make_async_copy(a, b, in_sem.at[i])
        for i, (a, b) in enumerate(((q_hbm, q_v), (g_hbm, g_v), (kv_hbm, kv_v), (lr_hbm, lr_v)))
    ]
    for c in loads:
        c.start()

    col = lax.broadcasted_iota(jnp.int32, (8, TQ), 1)
    lo = jnp.zeros((8, TQ), jnp.int32)
    hi = jnp.zeros((8, TQ), jnp.int32)
    start = jnp.int32(0)
    for k in range(NDOC):
        width = slen[0, k]
        hi = hi + jnp.where(col >= start, width, 0)
        start = start + tlen[0, k]
        lo = lo + jnp.where(col >= start, width, 0)
    lo = lo[0:1]
    hi = hi[0:1]

    loads[0].wait()
    loads[1].wait()
    zero = jnp.zeros((TQ, HS), F32)
    w1[0:TQ, :] = jnp.concatenate([q_v[...].astype(F32), zero], axis=1).astype(BF16)
    w1[TQ : 2 * TQ, :] = jnp.concatenate([zero, g_v[...].astype(F32)], axis=1).astype(BF16)
    loads[2].wait()

    row = lax.broadcasted_iota(jnp.int32, (ROWS, TQ), 0)

    def first(i, carry):
        total, weighted = carry
        base = pl.multiple_of(i * ROWS, ROWS)
        both = lax.dot_general(kv_v[pl.ds(base, ROWS), :], w1[...], NT, preferred_element_type=F32)
        dprob = both[:, TQ:]
        pos = row + base
        allowed = jnp.logical_and(pos >= lo, pos < hi)
        expo = jnp.where(allowed, jnp.exp(both[:, :TQ]), 0.0)
        expo_s[pl.ds(base, ROWS), :] = expo
        dprob_s[pl.ds(base, ROWS), :] = dprob
        return total + fold8(expo), weighted + fold8(expo * dprob)

    zeros = jnp.zeros((8, TQ), F32)
    total, weighted = lax.fori_loop(0, S // ROWS, first, (zeros, zeros))
    total = jnp.sum(total, axis=0, keepdims=True)
    delta = jnp.sum(weighted, axis=0, keepdims=True) / total
    scale = 1.0 / total

    def second(i, _):
        base = pl.multiple_of(i * ROWS, ROWS)
        prob = expo_s[pl.ds(base, ROWS), :] * scale
        ds = (prob * (dprob_s[pl.ds(base, ROWS), :] - delta)).astype(BF16)
        ds_s[pl.ds(base, ROWS), :] = ds
        both = jnp.concatenate([ds, prob.astype(BF16)], axis=1)
        grads = jnp.dot(both, w1[...], preferred_element_type=F32).astype(BF16)
        msg[pl.ds(pl.multiple_of(i * (ROWS // OWN), ROWS // OWN), ROWS // OWN)] = grads.reshape(
            ROWS // OWN, OWN, 2 * HS
        )
        return 0

    lax.fori_loop(0, S // ROWS, second, 0)

    loads[3].wait()
    lr = lr_v[...].astype(F32)
    packed = jnp.concatenate([lr[8 * j : 8 * j + 8] for j in range(4)], axis=1).astype(BF16)
    lr_all[pl.ds(m, 1)] = packed.reshape(1, 8, 4 * RANK2)

    pl.semaphore_wait(barrier, MP - 1 + DP - self_adapter.astype(jnp.int32))

    def lr_z(s, _):
        peer = x * ZS + (z + s) % ZS
        pltpu.make_async_remote_copy(
            src_ref=lr_all.at[m], dst_ref=lr_all.at[m], send_sem=lrz_send, recv_sem=lrz_recv,
            device_id=(p, peer), device_id_type=MESH,
        ).start()
        return 0

    lax.fori_loop(1, ZS, lr_z, 0)

    def send(s, _):
        peer = ((x + (s + 1) % XS) % XS) * ZS + (z + far_first(s // XS)) % ZS
        pltpu.make_async_remote_copy(
            src_ref=msg.at[peer], dst_ref=recv.at[m], send_sem=send_sem, recv_sem=recv_sem,
            device_id=(p, peer), device_id_type=MESH,
        ).start()
        return 0

    own = pltpu.make_async_copy(msg.at[m], recv.at[m], own_sem.at[0])
    own.start()
    lax.fori_loop(0, 24, send, 0)

    qg_out[...] = lax.dot_general(ds_s[...], kv_v[...], TN, preferred_element_type=F32)[:, :HS].astype(BF16)

    def wait_bytes(ref, count, sem):
        pltpu.make_async_copy(ref.at[pl.ds(0, count)], ref.at[pl.ds(0, count)], sem).wait()

    wait_bytes(lr_all, ZS - 1, lrz_recv)
    mine = lr_all.at[pl.ds(pl.multiple_of(x * ZS, ZS), ZS)]
    for j in range(1, XS):
        pltpu.make_async_remote_copy(
            src_ref=mine, dst_ref=mine, send_sem=lrx_send, recv_sem=lrx_recv,
            device_id=(p, ((x + j) % XS) * ZS + z), device_id_type=MESH,
        ).start()

    lax.fori_loop(24, 44, send, 0)

    wait_bytes(lr_all, ZS * (XS - 1), lrx_recv)
    gathered = lr_all[...].astype(F32)
    for j in range(4):
        lr_full[:, 8 * j : 8 * j + 8, :] = pltpu.roll(
            gathered.reshape(MP * 8, 4 * RANK2), (4 - j) % 4 * RANK2, axis=1
        ).reshape(MP, 8, 4 * RANK2)
    terms = lax.dot_general(
        msg[...].reshape(S, 2 * HS), lr_full[...].reshape(S, 4 * RANK2).astype(BF16), TN,
        preferred_element_type=F32,
    )
    lane = lax.broadcasted_iota(jnp.int32, (HS, 4 * RANK2), 1)
    adapter_send[...] = jnp.where(lane < RANK2 // 2, terms[:HS], terms[HS:]).reshape(8, 8, 4 * RANK2)

    for k in range(8):
        dst_mp = 8 * gb + k
        me = jnp.logical_and(p == ga, dst_mp == m)

        @pl.when(jnp.logical_not(me))
        def _():
            pltpu.make_async_remote_copy(
                src_ref=adapter_send.at[k], dst_ref=adapter_recv.at[p], send_sem=ad_send, recv_sem=ad_recv,
                device_id=(ga, dst_mp), device_id_type=MESH,
            ).start()

        @pl.when(me)
        def _():
            pltpu.make_async_copy(adapter_send.at[k], adapter_recv.at[p], own_sem.at[1]).start()

    lax.fori_loop(44, MP - 1, send, 0)

    own.wait()
    wait_bytes(lr_all, ZS - 1, lrz_send)
    wait_bytes(lr_all, ZS * (XS - 1), lrx_send)

    @pl.when(self_adapter)
    def _():
        wait_bytes(adapter_send, 1, own_sem.at[1])
        wait_bytes(adapter_send, 7, ad_send)
        wait_bytes(adapter_recv, 7, ad_recv)

    @pl.when(jnp.logical_not(self_adapter))
    def _():
        wait_bytes(adapter_send, 8, ad_send)
        wait_bytes(adapter_recv, 8, ad_recv)

    wait_bytes(msg, MP - 1, send_sem)
    wait_bytes(recv, MP - 1, recv_sem)


def owner_kernel(recv, up, adapter_recv, qg_in, key_out, value_out, lrg_out, aug_out, qg_out):
    for j in range(MP // 2):
        a = recv[2 * j]
        b = recv[2 * j + 1]
        key_out[:, 128 * j : 128 * j + 128] = jnp.concatenate([a[:, :HS], b[:, :HS]], axis=1)
        value_out[:, 128 * j : 128 * j + 128] = jnp.concatenate([a[:, HS:], b[:, HS:]], axis=1)
    from_key = lax.dot_general(key_out[...], up[...], NT, preferred_element_type=F32)
    from_value = lax.dot_general(value_out[...], up[...], NT, preferred_element_type=F32)
    lane = lax.broadcasted_iota(jnp.int32, (OWN, RANK2), 1)
    lrg_out[...] = ADAPTER_FACTOR * jnp.where(lane < RANK2 // 2, from_key, from_value)
    aug_out[...] = ADAPTER_FACTOR * jnp.sum(adapter_recv[...], axis=0)[:, :RANK2]
    qg_out[...] = qg_in[...]


def local(query, kv_cache, out_grad, source_lengths, target_lengths, low_rank, adapter_up_matrix):
    any_spec = pl.BlockSpec(memory_space=pl.ANY)
    smem = pl.BlockSpec(memory_space=pltpu.SMEM)
    vmem = pl.BlockSpec(memory_space=pltpu.VMEM)
    recv, adapter_recv, qg = pl.pallas_call(
        exchange_kernel,
        out_shape=(
            jax.ShapeDtypeStruct((MP, OWN, 2 * HS), BF16),
            jax.ShapeDtypeStruct((DP, 8, 4 * RANK2), F32),
            jax.ShapeDtypeStruct((TQ, HS), BF16),
        ),
        in_specs=[any_spec, any_spec, any_spec, smem, smem, any_spec],
        out_specs=(any_spec, any_spec, vmem),
        scratch_shapes=[
            pltpu.VMEM((TQ, HS), BF16),
            pltpu.VMEM((S, 2 * HS), BF16),
            pltpu.VMEM((TQ, HS), BF16),
            pltpu.VMEM((OWN, RANK2), BF16),
            pltpu.VMEM((2 * TQ, 2 * HS), BF16),
            pltpu.VMEM((S, TQ), F32),
            pltpu.VMEM((S, TQ), F32),
            pltpu.VMEM((S, TQ), BF16),
            pltpu.VMEM((MP, OWN, 2 * HS), BF16),
            pltpu.VMEM((MP, 8, 4 * RANK2), BF16),
            pltpu.VMEM((MP, OWN, 4 * RANK2), F32),
            pltpu.VMEM((8, 8, 4 * RANK2), F32),
            pltpu.SemaphoreType.DMA((4,)),
            pltpu.SemaphoreType.DMA,
            pltpu.SemaphoreType.DMA,
            pltpu.SemaphoreType.DMA,
            pltpu.SemaphoreType.DMA,
            pltpu.SemaphoreType.DMA,
            pltpu.SemaphoreType.DMA,
            pltpu.SemaphoreType.DMA,
            pltpu.SemaphoreType.DMA,
            pltpu.SemaphoreType.DMA((2,)),
        ],
        compiler_params=pltpu.CompilerParams(
            collective_id=0, has_side_effects=True, vmem_limit_bytes=40 << 20
        ),
        name="exchange",
    )(query, kv_cache, out_grad, source_lengths, target_lengths, low_rank)
    key_gradient, value_grad, low_rank_gradient, adapter_up_gradient, query_grad = pl.pallas_call(
        owner_kernel,
        out_shape=(
            jax.ShapeDtypeStruct((OWN, MP * HS), BF16),
            jax.ShapeDtypeStruct((OWN, MP * HS), BF16),
            jax.ShapeDtypeStruct((OWN, RANK2), F32),
            jax.ShapeDtypeStruct((8, RANK2), F32),
            jax.ShapeDtypeStruct((TQ, HS), BF16),
        ),
        in_specs=[vmem] * 4,
        out_specs=(vmem,) * 5,
        name="owner",
    )(recv, adapter_up_matrix, adapter_recv, qg)
    return query_grad, key_gradient, value_grad, low_rank_gradient, adapter_up_gradient


def solution(mesh):
    in_specs = (
        P("dp", "mp"),
        P("dp", "mp"),
        P("dp", "mp"),
        P("dp", None),
        P("dp", None),
        P(("dp", "mp"), None),
        P(),
    )
    out_specs = (
        P("dp", "mp"),
        P(("dp", "mp"), None),
        P(("dp", "mp"), None),
        P(("dp", "mp"), None),
        P(("dp", "mp"), None),
    )
    return jax.shard_map(local, mesh=mesh, in_specs=in_specs, out_specs=out_specs, check_vma=False)
```

time: 543 us -> 57.4 us (0.11)
  waiting for transfers between devices: 487 us -> 0 us
  Pallas kernels: 0 us -> 50.2 us
  starting transfers between devices: 19.1 us -> 0 us
  between operations: 14.3 us -> 0.7 us
  matrix products: 7.89 us -> 0 us
    unnamed x2 -> x0, waiting for transfers between devices: 458 us -> none
    pallas_call x0 -> x2, Pallas kernels: none -> 50.2 us  [the longest x1 48 us: local(): pl.pallas_call(exchange_kernel, out_shape=(jax.ShapeDtypeStruct((MP, OWN,...]
    all_to_all x1 -> x0, waiting for transfers between devices: 28.8 us -> none  [local(): lax.all_to_all(stacked, 'mp', split_axis=1, concat_axis=2, tiled=True)]
    all_to_all x1 -> x0, starting transfers between devices: 19.1 us -> none  [local(): lax.all_to_all(stacked, 'mp', split_axis=1, concat_axis=2, tiled=True)]
    dot_general x32 -> x0, matrix products: 7.89 us -> none  [the longest x8 2.38 us: tile_terms(): jnp.einsum('qhd,khd->hqk', query_rows, key_rows, preferred_element_type=j...]
  transfers between devices with their start and end apart: 2 -> 0, of which waited for: 2 -> 0; matrix products, arithmetic and copies ran while one was open for 0% -> 0% of each run, Pallas kernels for 0% -> 0%
where the time goes in v1:
time: 57.4 us; the launch traced here: 57.1 us
  Pallas kernels  50.2 us (87%)
  local copies, waits for them, and re-layouts  6.17 us (11%)
  between operations  0.7 us (1%)
    pallas_call x1, Pallas kernels, local(): pl.pallas_call(exchange_kernel, out_shape=(jax.ShapeDtypeStruct((MP, OWN,...  48 us
    unnamed x19, local copies, waits for them, and re-layouts  6.17 us
    pallas_call x1, Pallas kernels, local(): pl.pallas_call(owner_kernel, out_shape=(jax.ShapeDtypeStruct((OWN, MP * H...  2.21 us

profile of v1, /device:TPU:1, one launch (start us, length us, event | category | flops | bytes accessed | tf_op | source)
XLA Modules:
  0.0 57.1 jit_solution(10032582096837962205)
XLA Ops:
  0.6 0.0 copy-start.7
  0.6 0.9 %copy.12.q_hbm = bf16[256,64]{1,0:T(8,128)(2,1)S(1)} copy(bf16[256,64]{0,1:T(8,128)(2,1)} %param.7) | data formatting | bytes 65536 | tf_op args[0]
  1.5 0.0 copy-done.7
  1.5 0.0 copy-start.4
  1.5 0.0 copy-start.5
  1.6 0.0 copy-start.6
  1.6 0.1 copy.13.g_hbm
  1.7 0.5 copy-done.4
  2.2 0.0 copy-done.5
  2.2 0.0 copy-done.6
  2.2 0.0 copy-start.1
  2.2 1.0 %copy-done.1 = bf16[2048,128]{1,0:T(8,128)(2,1)S(1)} copy-done((bf16[2048,128]{1,0:T(8,128)(2,1)S(1)}, bf16[2048,128]{1,0:T(8,128)(2,1)}, u32[]{:S(2)}) %copy-start.1) | copy-done | bytes 524312
  3.3 48.0 %exchange.1 = (bf16[64,32,128]{2,1,0:T(8,128)(2,1)S(1)}, f32[8,8,128]{2,1,0:T(8,128)S(1)}, bf16[256,64]{1,0:T(8,128)(2,1)S(1)}) custom-call(bf16[256,64]{1,0:T(8,128)(2,1)S(1)} %copy.12.q_hbm, bf16[2048,128]{1,0:T(8,128)(2,1)S(1)} %copy-done.1, bf16[256,64]{1,0:T(8,128)(2,1)S(1)} %copy.13.g_hbm, s32[1,8]{1,0:T(1,128)S(1)} %copy-done.5, ...), custom_call_target="tpu_custom_call" | custom-call | tf_op jit(solution)/shard_map/exchange/pallas_call | solution.py:237
  51.3 0.0 copy-start
  51.3 0.8 %copy-done = bf16[64,32,128]{2,1,0:T(8,128)(2,1)} copy-done((bf16[64,32,128]{2,1,0:T(8,128)(2,1)}, bf16[64,32,128]{2,1,0:T(8,128)(2,1)S(1)}, u32[]{:S(2)}) %copy-start) | copy-done | bytes 524312
  52.1 0.0 copy-start.2
  52.1 0.6 %copy-done.2 = bf16[256,64]{1,0:T(8,128)(2,1)} copy-done((bf16[256,64]{1,0:T(8,128)(2,1)}, bf16[256,64]{1,0:T(8,128)(2,1)S(1)}, u32[]{:S(2)}) %copy-start.2) | copy-done | bytes 32792
  52.7 0.0 copy-start.3
  52.7 0.6 %copy-done.3 = f32[8,8,128]{2,1,0:T(8,128)} copy-done((f32[8,8,128]{2,1,0:T(8,128)}, f32[8,8,128]{2,1,0:T(8,128)S(1)}, u32[]{:S(2)}) %copy-start.3) | copy-done | bytes 32792
  53.3 2.2 %owner.1 = (bf16[32,4096]{1,0:T(8,128)(2,1)}, bf16[32,4096]{1,0:T(8,128)(2,1)}, f32[32,32]{1,0:T(8,128)}, f32[8,32]{1,0:T(8,128)}, bf16[256,64]{1,0:T(8,128)(2,1)}) custom-call(bf16[64,32,128]{2,1,0:T(8,128)(2,1)} %copy-done, bf16[32,4096]{1,0:T(8,128)(2,1)} %up.1, f32[8,8,128]{2,1,0:T(8,128)} %copy-done.3, bf16[256,64]{1,0:T(8,128)(2,1)} %copy-done.2), custom_call_target="tpu_custom_call" | custom-call | tf_op jit(solution)/shard_map/owner/pallas_call | solution.py:275
  55.5 1.5 %copy.14 = bf16[256,64]{0,1:T(8,128)(2,1)} copy(bf16[256,64]{1,0:T(8,128)(2,1)} %get-tuple-element.21) | data formatting | bytes 65536
Async XLA Ops:
  0.6 0.9 %copy-start.7 = (bf16[256,64]{0,1:T(8,128)(2,1)S(1)}, bf16[256,64]{0,1:T(8,128)(2,1)}, u32[]{:S(2)}) copy-start(bf16[256,64]{0,1:T(8,128)(2,1)} %param.9) | copy-start | bytes 98308
  1.5 0.7 %copy-start.4 = (bf16[32,32]{1,0:T(8,128)(2,1)S(1)}, bf16[32,32]{1,0:T(8,128)(2,1)}, u32[]{:S(2)}) copy-start(bf16[32,32]{1,0:T(8,128)(2,1)} %lr_hbm.1) | copy-start | bytes 6148
  1.5 0.7 %copy-start.5 = (s32[1,8]{1,0:T(1,128)S(1)}, s32[1,8]{1,0:T(1,128)}, u32[]{:S(2)}) copy-start(s32[1,8]{1,0:T(1,128)} %slen.1) | copy-start | bytes 100
  1.6 0.7 %copy-start.6 = (s32[1,8]{1,0:T(1,128)S(1)}, s32[1,8]{1,0:T(1,128)}, u32[]{:S(2)}) copy-start(s32[1,8]{1,0:T(1,128)} %tlen.1) | copy-start | bytes 100
  2.2 1.0 %copy-start.1 = (bf16[2048,128]{1,0:T(8,128)(2,1)S(1)}, bf16[2048,128]{1,0:T(8,128)(2,1)}, u32[]{:S(2)}) copy-start(bf16[2048,128]{1,0:T(8,128)(2,1)} %kv_hbm.1) | copy-start | bytes 1572868
  51.3 0.8 %copy-start = (bf16[64,32,128]{2,1,0:T(8,128)(2,1)}, bf16[64,32,128]{2,1,0:T(8,128)(2,1)S(1)}, u32[]{:S(2)}) copy-start(bf16[64,32,128]{2,1,0:T(8,128)(2,1)S(1)} %get-tuple-element.13.recv) | copy-start | bytes 1572868
  52.1 0.6 %copy-start.2 = (bf16[256,64]{1,0:T(8,128)(2,1)}, bf16[256,64]{1,0:T(8,128)(2,1)S(1)}, u32[]{:S(2)}) copy-start(bf16[256,64]{1,0:T(8,128)(2,1)S(1)} %get-tuple-element.15.qg_in) | copy-start | bytes 98308
  52.7 0.6 %copy-start.3 = (f32[8,8,128]{2,1,0:T(8,128)}, f32[8,8,128]{2,1,0:T(8,128)S(1)}, u32[]{:S(2)}) copy-start(f32[8,8,128]{2,1,0:T(8,128)S(1)} %get-tuple-element.14.adapter_recv) | copy-start | bytes 98308

commit v2 on v1

--- a/solution.py
+++ b/solution.py
@@ -18,6 +18,7 @@
 RANK2 = 32
 ROWS = 256
 ADAPTER_FACTOR = 2.0
+VMEM_LIMIT = 63 << 20
 MESH = pl.DeviceIdType.MESH
 F32 = jnp.float32
 BF16 = jnp.bfloat16
@@ -37,7 +38,7 @@
 def exchange_kernel(
     q_hbm, kv_hbm, g_hbm, slen, tlen, lr_hbm,
     recv, adapter_recv, qg_out,
-    q_v, kv_v, g_v, lr_v, w1, expo_s, dprob_s, ds_s, msg, lr_all, lr_full, adapter_send,
+    kv_v, lr_v, w1, expo_s, dprob_s, ds_s, msg, lr_all, lr_full, adapter_send,
     in_sem, send_sem, recv_sem, lrz_send, lrz_recv, lrx_send, lrx_recv, ad_send, ad_recv, own_sem,
 ):
     p = lax.axis_index("dp")
@@ -65,7 +66,14 @@
 
     loads = [
         pltpu.make_async_copy(a, b, in_sem.at[i])
-        for i, (a, b) in enumerate(((q_hbm, q_v), (g_hbm, g_v), (kv_hbm, kv_v), (lr_hbm, lr_v)))
+        for i, (a, b) in enumerate(
+            (
+                (q_hbm, w1.at[0:HS, 0:TQ]),
+                (g_hbm, w1.at[HS : 2 * HS, TQ : 2 * TQ]),
+                (kv_hbm, kv_v),
+                (lr_hbm, lr_v),
+            )
+        )
     ]
     for c in loads:
         c.start()
@@ -82,11 +90,11 @@
     lo = lo[0:1]
     hi = hi[0:1]
 
+    zero = jnp.zeros((HS, TQ), BF16)
+    w1[0:HS, TQ : 2 * TQ] = zero
+    w1[HS : 2 * HS, 0:TQ] = zero
     loads[0].wait()
     loads[1].wait()
-    zero = jnp.zeros((TQ, HS), F32)
-    w1[0:TQ, :] = jnp.concatenate([q_v[...].astype(F32), zero], axis=1).astype(BF16)
-    w1[TQ : 2 * TQ, :] = jnp.concatenate([zero, g_v[...].astype(F32)], axis=1).astype(BF16)
     loads[2].wait()
 
     row = lax.broadcasted_iota(jnp.int32, (ROWS, TQ), 0)
@@ -94,7 +102,7 @@
     def first(i, carry):
         total, weighted = carry
         base = pl.multiple_of(i * ROWS, ROWS)
-        both = lax.dot_general(kv_v[pl.ds(base, ROWS), :], w1[...], NT, preferred_element_type=F32)
+        both = jnp.dot(kv_v[pl.ds(base, ROWS), :], w1[...], preferred_element_type=F32)
         dprob = both[:, TQ:]
         pos = row + base
         allowed = jnp.logical_and(pos >= lo, pos < hi)
@@ -115,7 +123,7 @@
         ds = (prob * (dprob_s[pl.ds(base, ROWS), :] - delta)).astype(BF16)
         ds_s[pl.ds(base, ROWS), :] = ds
         both = jnp.concatenate([ds, prob.astype(BF16)], axis=1)
-        grads = jnp.dot(both, w1[...], preferred_element_type=F32).astype(BF16)
+        grads = lax.dot_general(both, w1[...], NT, preferred_element_type=F32).astype(BF16)
         msg[pl.ds(pl.multiple_of(i * (ROWS // OWN), ROWS // OWN), ROWS // OWN)] = grads.reshape(
             ROWS // OWN, OWN, 2 * HS
         )
@@ -152,7 +160,7 @@
     own.start()
     lax.fori_loop(0, 24, send, 0)
 
-    qg_out[...] = lax.dot_general(ds_s[...], kv_v[...], TN, preferred_element_type=F32)[:, :HS].astype(BF16)
+    qg_out[...] = lax.dot_general(kv_v[...], ds_s[...], TN, preferred_element_type=F32)[:HS].astype(BF16)
 
     def wait_bytes(ref, count, sem):
         pltpu.make_async_copy(ref.at[pl.ds(0, count)], ref.at[pl.ds(0, count)], sem).wait()
@@ -239,16 +247,14 @@
         out_shape=(
             jax.ShapeDtypeStruct((MP, OWN, 2 * HS), BF16),
             jax.ShapeDtypeStruct((DP, 8, 4 * RANK2), F32),
-            jax.ShapeDtypeStruct((TQ, HS), BF16),
+            jax.ShapeDtypeStruct((HS, TQ), BF16),
         ),
         in_specs=[any_spec, any_spec, any_spec, smem, smem, any_spec],
         out_specs=(any_spec, any_spec, vmem),
         scratch_shapes=[
-            pltpu.VMEM((TQ, HS), BF16),
             pltpu.VMEM((S, 2 * HS), BF16),
-            pltpu.VMEM((TQ, HS), BF16),
             pltpu.VMEM((OWN, RANK2), BF16),
-            pltpu.VMEM((2 * TQ, 2 * HS), BF16),
+            pltpu.VMEM((2 * HS, 2 * TQ), BF16),
             pltpu.VMEM((S, TQ), F32),
             pltpu.VMEM((S, TQ), F32),
             pltpu.VMEM((S, TQ), BF16),
@@ -268,10 +274,10 @@
             pltpu.SemaphoreType.DMA((2,)),
         ],
         compiler_params=pltpu.CompilerParams(
-            collective_id=0, has_side_effects=True, vmem_limit_bytes=40 << 20
+            collective_id=0, has_side_effects=True, vmem_limit_bytes=VMEM_LIMIT
         ),
         name="exchange",
-    )(query, kv_cache, out_grad, source_lengths, target_lengths, low_rank)
+    )(query.T, kv_cache, out_grad.T, source_lengths, target_lengths, low_rank)
     key_gradient, value_grad, low_rank_gradient, adapter_up_gradient, query_grad = pl.pallas_call(
         owner_kernel,
         out_shape=(
@@ -279,13 +285,14 @@
             jax.ShapeDtypeStruct((OWN, MP * HS), BF16),
             jax.ShapeDtypeStruct((OWN, RANK2), F32),
             jax.ShapeDtypeStruct((8, RANK2), F32),
-            jax.ShapeDtypeStruct((TQ, HS), BF16),
+            jax.ShapeDtypeStruct((HS, TQ), BF16),
         ),
         in_specs=[vmem] * 4,
         out_specs=(vmem,) * 5,
+        compiler_params=pltpu.CompilerParams(vmem_limit_bytes=VMEM_LIMIT),
         name="owner",
     )(recv, adapter_up_matrix, adapter_recv, qg)
-    return query_grad, key_gradient, value_grad, low_rank_gradient, adapter_up_gradient
+    return query_grad.T, key_gradient, value_grad, low_rank_gradient, adapter_up_gradient
 
 
 def solution(mesh):

time: 57.4 us -> 51.9 us (0.904)
  local copies, waits for them, and re-layouts: 6.17 us -> 0 us
  Pallas kernels: 50.2 us -> 51.1 us
    unnamed x19 -> x0, local copies, waits for them, and re-layouts: 6.17 us -> none
    pallas_call x1, Pallas kernels: 48 us -> 48.9 us  [local(): pl.pallas_call(exchange_kernel, out_shape=(jax.ShapeDtypeStruct((MP, OWN,...]
where the time goes in v2:
time: 51.9 us; the launch traced here: 51.7 us
  Pallas kernels  51.1 us (98%)
  between operations  0.64 us (1%)
    pallas_call x1, Pallas kernels, local(): pl.pallas_call(exchange_kernel, out_shape=(jax.ShapeDtypeStruct((MP, OWN,...  48.9 us
    pallas_call x1, Pallas kernels, local(): pl.pallas_call(owner_kernel, out_shape=(jax.ShapeDtypeStruct((OWN, MP * H...  2.2 us

profile of v2, /device:TPU:1, one launch (start us, length us, event | category | flops | bytes accessed | tf_op | source)
XLA Modules:
  0.0 51.7 jit_solution(9613143881578724781)
XLA Ops:
  0.6 48.9 %exchange.1 = (bf16[64,32,128]{2,1,0:T(8,128)(2,1)}, f32[8,8,128]{2,1,0:T(8,128)}, bf16[64,256]{1,0:T(8,128)(2,1)}) custom-call(bf16[64,256]{1,0:T(8,128)(2,1)} %bitcast.3, bf16[2048,128]{1,0:T(8,128)(2,1)} %kv_hbm.1, bf16[64,256]{1,0:T(8,128)(2,1)} %bitcast.4, s32[1,8]{1,0:T(1,128)} %slen.1, s32[1,8]{1,0:T(1,128)} %tlen.1, bf16[32,32]{1,0:T(8,128)(2,1)} %lr_hbm.1), custom_call_target="tpu_custom_call" | custom-call | tf_op jit(solution)/shard_map/exchange/pallas_call | solution.py:245
  49.5 2.2 %owner.1 = (bf16[32,4096]{1,0:T(8,128)(2,1)}, bf16[32,4096]{1,0:T(8,128)(2,1)}, f32[32,32]{1,0:T(8,128)}, f32[8,32]{1,0:T(8,128)}, bf16[64,256]{1,0:T(8,128)(2,1)}) custom-call(bf16[64,32,128]{2,1,0:T(8,128)(2,1)} %get-tuple-element.13.recv, bf16[32,4096]{1,0:T(8,128)(2,1)} %up.1, f32[8,8,128]{2,1,0:T(8,128)} %get-tuple-element.14.adapter_recv, ...), custom_call_target="tpu_custom_call" | custom-call | tf_op jit(solution)/shard_map/owner/pallas_call | solution.py:281

commit v3 on v2

--- a/solution.py
+++ b/solution.py
@@ -30,33 +30,32 @@
     return jnp.sum(x.reshape(x.shape[0] // 8, 8, x.shape[1]), axis=0)
 
 
-def far_first(u):
-    half = (u + 1) // 2
-    return jnp.where(u % 2 == 1, 8 - half, 8 + half) % ZS
+Z_ORDER = (8, 1, 15, 7, 9, 2, 14, 6, 10, 3, 13, 5, 11, 4, 12, 0)
+ORDER = [(dx, dz) for dx in (2, 1, 3, 0) for dz in Z_ORDER if (dx, dz) != (0, 0)]
 
 
 def exchange_kernel(
     q_hbm, kv_hbm, g_hbm, slen, tlen, lr_hbm,
     recv, adapter_recv, qg_out,
-    kv_v, lr_v, w1, expo_s, dprob_s, ds_s, msg, lr_all, lr_full, adapter_send,
+    kv_v, lr_v, w1, expo_s, dprob_s, ds_s, msg, lr_all, lr_full, term_s, adapter_send,
     in_sem, send_sem, recv_sem, lrz_send, lrz_recv, lrx_send, lrx_recv, ad_send, ad_recv, own_sem,
 ):
     p = lax.axis_index("dp")
     m = lax.axis_index("mp")
-    x = m // ZS
-    z = m % ZS
-    ga = m // 8
-    gb = m % 8
+    x = lax.div(m, ZS)
+    z = lax.rem(m, ZS)
+    ga = lax.div(m, 8)
+    gb = lax.rem(m, 8)
     self_adapter = jnp.logical_and(p == ga, gb == ga)
 
     barrier = pltpu.get_barrier_semaphore()
 
-    def greet(s, _):
-        pl.semaphore_signal(barrier, inc=1, device_id=(p, (m + s) % MP), device_id_type=MESH)
-        return 0
-
-    lax.fori_loop(1, MP, greet, 0)
-    src_head = 8 * p + m // 8
+    def peer_of(dx, dz):
+        return lax.rem(x + dx, XS) * ZS + lax.rem(z + dz, ZS)
+
+    for dx, dz in ORDER:
+        pl.semaphore_signal(barrier, inc=1, device_id=(p, peer_of(dx, dz)), device_id_type=MESH)
+    src_head = 8 * p + ga
     for j in range(DP):
         not_me = jnp.logical_not(jnp.logical_and(p == j, src_head == m))
 
@@ -138,27 +137,23 @@
 
     pl.semaphore_wait(barrier, MP - 1 + DP - self_adapter.astype(jnp.int32))
 
-    def lr_z(s, _):
-        peer = x * ZS + (z + s) % ZS
+    for dz in Z_ORDER[:-1]:
         pltpu.make_async_remote_copy(
             src_ref=lr_all.at[m], dst_ref=lr_all.at[m], send_sem=lrz_send, recv_sem=lrz_recv,
-            device_id=(p, peer), device_id_type=MESH,
+            device_id=(p, peer_of(0, dz)), device_id_type=MESH,
         ).start()
-        return 0
-
-    lax.fori_loop(1, ZS, lr_z, 0)
-
-    def send(s, _):
-        peer = ((x + (s + 1) % XS) % XS) * ZS + (z + far_first(s // XS)) % ZS
-        pltpu.make_async_remote_copy(
-            src_ref=msg.at[peer], dst_ref=recv.at[m], send_sem=send_sem, recv_sem=recv_sem,
-            device_id=(p, peer), device_id_type=MESH,
-        ).start()
-        return 0
+
+    def send(first_one, last_one):
+        for dx, dz in ORDER[first_one:last_one]:
+            peer = peer_of(dx, dz)
+            pltpu.make_async_remote_copy(
+                src_ref=msg.at[peer], dst_ref=recv.at[m], send_sem=send_sem, recv_sem=recv_sem,
+                device_id=(p, peer), device_id_type=MESH,
+            ).start()
 
     own = pltpu.make_async_copy(msg.at[m], recv.at[m], own_sem.at[0])
     own.start()
-    lax.fori_loop(0, 24, send, 0)
+    send(0, 24)
 
     qg_out[...] = lax.dot_general(kv_v[...], ds_s[...], TN, preferred_element_type=F32)[:HS].astype(BF16)
 
@@ -167,13 +162,13 @@
 
     wait_bytes(lr_all, ZS - 1, lrz_recv)
     mine = lr_all.at[pl.ds(pl.multiple_of(x * ZS, ZS), ZS)]
-    for j in range(1, XS):
+    for j in (2, 1, 3):
         pltpu.make_async_remote_copy(
             src_ref=mine, dst_ref=mine, send_sem=lrx_send, recv_sem=lrx_recv,
-            device_id=(p, ((x + j) % XS) * ZS + z), device_id_type=MESH,
+            device_id=(p, peer_of(j, 0)), device_id_type=MESH,
         ).start()
 
-    lax.fori_loop(24, 44, send, 0)
+    send(24, 40)
 
     wait_bytes(lr_all, ZS * (XS - 1), lrx_recv)
     gathered = lr_all[...].astype(F32)
@@ -186,7 +181,15 @@
         preferred_element_type=F32,
     )
     lane = lax.broadcasted_iota(jnp.int32, (HS, 4 * RANK2), 1)
-    adapter_send[...] = jnp.where(lane < RANK2 // 2, terms[:HS], terms[HS:]).reshape(8, 8, 4 * RANK2)
+    term_s[...] = jnp.where(lane < RANK2 // 2, terms[:HS], terms[HS:])
+    group = lax.broadcasted_iota(jnp.int32, (HS // 4, 4 * RANK2), 1) // RANK2
+    full = term_s[pl.ds(0, HS // 4, stride=4), :]
+    for j in range(1, 4):
+        full = jnp.where(
+            group == j, pltpu.roll(term_s[pl.ds(j, HS // 4, stride=4), :], j * RANK2, axis=1), full
+        )
+    for k in range(8):
+        adapter_send[k] = full[2 * k : 2 * k + 2]
 
     for k in range(8):
         dst_mp = 8 * gb + k
@@ -203,7 +206,7 @@
         def _():
             pltpu.make_async_copy(adapter_send.at[k], adapter_recv.at[p], own_sem.at[1]).start()
 
-    lax.fori_loop(44, MP - 1, send, 0)
+    send(40, MP - 1)
 
     own.wait()
     wait_bytes(lr_all, ZS - 1, lrz_send)
@@ -224,18 +227,54 @@
     wait_bytes(recv, MP - 1, recv_sem)
 
 
-def owner_kernel(recv, up, adapter_recv, qg_in, key_out, value_out, lrg_out, aug_out, qg_out):
-    for j in range(MP // 2):
-        a = recv[2 * j]
-        b = recv[2 * j + 1]
-        key_out[:, 128 * j : 128 * j + 128] = jnp.concatenate([a[:, :HS], b[:, :HS]], axis=1)
-        value_out[:, 128 * j : 128 * j + 128] = jnp.concatenate([a[:, HS:], b[:, HS:]], axis=1)
-    from_key = lax.dot_general(key_out[...], up[...], NT, preferred_element_type=F32)
-    from_value = lax.dot_general(value_out[...], up[...], NT, preferred_element_type=F32)
+def owner_kernel(
+    recv, up_hbm, adapter_recv, qg_in, key_out, value_out, lrg_out, aug_out, qg_out,
+    recv_v, grads, up, terms, qg_v, in_sem, out_sem, side_sem,
+):
+    parts = 4
+    heads = MP // parts
+    width = heads * HS
+    arrive = [
+        pltpu.make_async_copy(
+            recv.at[pl.ds(c * heads, heads)], recv_v.at[pl.ds(c * heads, heads)], in_sem.at[c]
+        )
+        for c in range(parts)
+    ]
+    side = [
+        pltpu.make_async_copy(a, b, side_sem.at[i])
+        for i, (a, b) in enumerate(((up_hbm, up), (adapter_recv, terms), (qg_in, qg_v)))
+    ]
+    for copy in arrive + side:
+        copy.start()
+    leave = []
+    for c in range(parts):
+        arrive[c].wait()
+        for j in range(c * heads // 2, (c + 1) * heads // 2):
+            a = recv_v[2 * j]
+            b = recv_v[2 * j + 1]
+            cols = slice(128 * j, 128 * j + 128)
+            grads[0:OWN, cols] = jnp.concatenate([a[:, :HS], b[:, :HS]], axis=1)
+            grads[OWN : 2 * OWN, cols] = jnp.concatenate([a[:, HS:], b[:, HS:]], axis=1)
+        cols = pl.ds(c * width, width)
+        for i, out in enumerate((key_out, value_out)):
+            copy = pltpu.make_async_copy(
+                grads.at[pl.ds(i * OWN, OWN), cols], out.at[:, cols], out_sem.at[2 * c + i]
+            )
+            copy.start()
+            leave.append(copy)
+    for copy in side:
+        copy.wait()
+    back = pltpu.make_async_copy(qg_v, qg_out, side_sem.at[3])
+    back.start()
+    total = ADAPTER_FACTOR * jnp.sum(terms[...], axis=0)
+    for r in range(8):
+        aug_out[r : r + 1, :] = total[r // 4 : r // 4 + 1, r % 4 * RANK2 : (r % 4 + 1) * RANK2]
+    both = lax.dot_general(grads[...], up[...], NT, preferred_element_type=F32)
     lane = lax.broadcasted_iota(jnp.int32, (OWN, RANK2), 1)
-    lrg_out[...] = ADAPTER_FACTOR * jnp.where(lane < RANK2 // 2, from_key, from_value)
-    aug_out[...] = ADAPTER_FACTOR * jnp.sum(adapter_recv[...], axis=0)[:, :RANK2]
-    qg_out[...] = qg_in[...]
+    lrg_out[...] = ADAPTER_FACTOR * jnp.where(lane < RANK2 // 2, both[:OWN], both[OWN:])
+    for copy in leave:
+        copy.wait()
+    back.wait()
 
 
 def local(query, kv_cache, out_grad, source_lengths, target_lengths, low_rank, adapter_up_matrix):
@@ -246,7 +285,7 @@
         exchange_kernel,
         out_shape=(
             jax.ShapeDtypeStruct((MP, OWN, 2 * HS), BF16),
-            jax.ShapeDtypeStruct((DP, 8, 4 * RANK2), F32),
+            jax.ShapeDtypeStruct((DP, 2, 4 * RANK2), F32),
             jax.ShapeDtypeStruct((HS, TQ), BF16),
         ),
         in_specs=[any_spec, any_spec, any_spec, smem, smem, any_spec],
@@ -261,7 +300,8 @@
             pltpu.VMEM((MP, OWN, 2 * HS), BF16),
             pltpu.VMEM((MP, 8, 4 * RANK2), BF16),
             pltpu.VMEM((MP, OWN, 4 * RANK2), F32),
-            pltpu.VMEM((8, 8, 4 * RANK2), F32),
+            pltpu.VMEM((HS, 4 * RANK2), F32),
+            pltpu.VMEM((8, 2, 4 * RANK2), F32),
             pltpu.SemaphoreType.DMA((4,)),
             pltpu.SemaphoreType.DMA,
             pltpu.SemaphoreType.DMA,
@@ -287,8 +327,18 @@
             jax.ShapeDtypeStruct((8, RANK2), F32),
             jax.ShapeDtypeStruct((HS, TQ), BF16),
         ),
-        in_specs=[vmem] * 4,
-        out_specs=(vmem,) * 5,
+        in_specs=[any_spec] * 4,
+        out_specs=(any_spec, any_spec, vmem, vmem, any_spec),
+        scratch_shapes=[
+            pltpu.VMEM((MP, OWN, 2 * HS), BF16),
+            pltpu.VMEM((2 * OWN, MP * HS), BF16),
+            pltpu.VMEM((RANK2, MP * HS), BF16),
+            pltpu.VMEM((DP, 2, 4 * RANK2), F32),
+            pltpu.VMEM((HS, TQ), BF16),
+            pltpu.SemaphoreType.DMA((4,)),
+            pltpu.SemaphoreType.DMA((8,)),
+            pltpu.SemaphoreType.DMA((4,)),
+        ],
         compiler_params=pltpu.CompilerParams(vmem_limit_bytes=VMEM_LIMIT),
         name="owner",
     )(recv, adapter_up_matrix, adapter_recv, qg)

time: 51.9 us -> 49.6 us (0.956)
  Pallas kernels: 51.1 us -> 48.8 us
    pallas_call x1, Pallas kernels: 48.9 us -> 46.1 us  [local(): pl.pallas_call(exchange_kernel, out_shape=(jax.ShapeDtypeStruct((MP, OWN,...]
    pallas_call x1, Pallas kernels: 2.2 us -> 2.73 us  [local(): pl.pallas_call(owner_kernel, out_shape=(jax.ShapeDtypeStruct((OWN, MP * H...]
where the time goes in v3:
time: 49.6 us; the launch traced here: 49.5 us
  Pallas kernels  48.8 us (98%)
  between operations  0.64 us (1%)
    pallas_call x1, Pallas kernels, local(): pl.pallas_call(exchange_kernel, out_shape=(jax.ShapeDtypeStruct((MP, OWN,...  46.1 us
    pallas_call x1, Pallas kernels, local(): pl.pallas_call(owner_kernel, out_shape=(jax.ShapeDtypeStruct((OWN, MP * H...  2.73 us

profile of v3, /device:TPU:1, one launch (start us, length us, event | category | flops | bytes accessed | tf_op | source)
XLA Modules:
  0.0 49.5 jit_solution(15784419282869427317)
XLA Ops:
  0.6 46.1 %exchange.1 = (bf16[64,32,128]{2,1,0:T(8,128)(2,1)}, f32[8,2,128]{2,1,0:T(2,128)}, bf16[64,256]{1,0:T(8,128)(2,1)}) custom-call(bf16[64,256]{1,0:T(8,128)(2,1)} %bitcast.3, bf16[2048,128]{1,0:T(8,128)(2,1)} %kv_hbm.1, bf16[64,256]{1,0:T(8,128)(2,1)} %bitcast.4, s32[1,8]{1,0:T(1,128)} %slen.1, s32[1,8]{1,0:T(1,128)} %tlen.1, bf16[32,32]{1,0:T(8,128)(2,1)} %lr_hbm.1), custom_call_target="tpu_custom_call" | custom-call | tf_op jit(solution)/shard_map/exchange/pallas_call | solution.py:284
  46.7 2.7 %owner.1 = (bf16[32,4096]{1,0:T(8,128)(2,1)}, bf16[32,4096]{1,0:T(8,128)(2,1)}, f32[32,32]{1,0:T(8,128)}, f32[8,32]{1,0:T(8,128)}, bf16[64,256]{1,0:T(8,128)(2,1)}) custom-call(bf16[64,32,128]{2,1,0:T(8,128)(2,1)} %get-tuple-element.13.recv, bf16[32,4096]{1,0:T(8,128)(2,1)} %up_hbm.1, f32[8,2,128]{2,1,0:T(2,128)} %get-tuple-element.14.adapter_recv, ...), custom_call_target="tpu_custom_call" | custom-call | tf_op jit(solution)/shard_map/owner/pallas_call | solution.py:321

commit v4 on v3

--- a/solution.py
+++ b/solution.py
@@ -18,7 +18,8 @@
 RANK2 = 32
 ROWS = 256
 ADAPTER_FACTOR = 2.0
-VMEM_LIMIT = 63 << 20
+VMEM_LIMIT = 67_043_328 - (720 << 10)
+LEAVE_VMEM = 67_043_328 - (720 << 10)
 MESH = pl.DeviceIdType.MESH
 F32 = jnp.float32
 BF16 = jnp.bfloat16
@@ -35,9 +36,9 @@
 
 
 def exchange_kernel(
-    q_hbm, kv_hbm, g_hbm, slen, tlen, lr_hbm,
-    recv, adapter_recv, qg_out,
-    kv_v, lr_v, w1, expo_s, dprob_s, ds_s, msg, lr_all, lr_full, term_s, adapter_send,
+    q_hbm, kv_hbm, g_hbm, slen, tlen, lr_hbm, up_hbm,
+    grads, lrg_out, aug_out, qg_out,
+    kv_v, lr_v, up, w1, expo_s, dprob_s, ds_s, msg, lr_all, lr_full, term_s, adapter_send, recv, adapter_recv,
     in_sem, send_sem, recv_sem, lrz_send, lrz_recv, lrx_send, lrx_recv, ad_send, ad_recv, own_sem,
 ):
     p = lax.axis_index("dp")
@@ -71,6 +72,7 @@
                 (g_hbm, w1.at[HS : 2 * HS, TQ : 2 * TQ]),
                 (kv_hbm, kv_v),
                 (lr_hbm, lr_v),
+                (up_hbm, up),
             )
         )
     ]
@@ -147,13 +149,12 @@
         for dx, dz in ORDER[first_one:last_one]:
             peer = peer_of(dx, dz)
             pltpu.make_async_remote_copy(
-                src_ref=msg.at[peer], dst_ref=recv.at[m], send_sem=send_sem, recv_sem=recv_sem,
+                src_ref=msg.at[peer], dst_ref=recv.at[m], send_sem=send_sem, recv_sem=recv_sem.at[dx],
                 device_id=(p, peer), device_id_type=MESH,
             ).start()
 
-    own = pltpu.make_async_copy(msg.at[m], recv.at[m], own_sem.at[0])
-    own.start()
-    send(0, 24)
+    recv[pl.ds(m, 1)] = msg[pl.ds(m, 1)]
+    send(0, 36)
 
     qg_out[...] = lax.dot_general(kv_v[...], ds_s[...], TN, preferred_element_type=F32)[:HS].astype(BF16)
 
@@ -168,7 +169,7 @@
             device_id=(p, peer_of(j, 0)), device_id_type=MESH,
         ).start()
 
-    send(24, 40)
+    send(36, 50)
 
     wait_bytes(lr_all, ZS * (XS - 1), lrx_recv)
     gathered = lr_all[...].astype(F32)
@@ -204,17 +205,34 @@
 
         @pl.when(me)
         def _():
-            pltpu.make_async_copy(adapter_send.at[k], adapter_recv.at[p], own_sem.at[1]).start()
-
-    send(40, MP - 1)
-
-    own.wait()
+            pltpu.make_async_copy(adapter_send.at[k], adapter_recv.at[p], own_sem).start()
+
+    send(50, MP - 1)
+
+    loads[4].wait()
+
+    def place(dx):
+        wait_bytes(recv, ZS if dx else ZS - 1, recv_sem.at[dx])
+        column = lax.rem(x + XS - dx, XS)
+        for j in range(ZS // 2):
+            a = recv[column * ZS + 2 * j]
+            b = recv[column * ZS + 2 * j + 1]
+            lanes = pl.ds(pl.multiple_of(column * (ZS * HS) + 128 * j, 128), 128)
+            grads[0:OWN, lanes] = jnp.concatenate([a[:, :HS], b[:, :HS]], axis=1)
+            grads[OWN : 2 * OWN, lanes] = jnp.concatenate([a[:, HS:], b[:, HS:]], axis=1)
+        lanes = pl.ds(pl.multiple_of(column * (ZS * HS), ZS * HS), ZS * HS)
+        return lax.dot_general(grads[:, lanes], up[:, lanes], NT, preferred_element_type=F32)
+
+    both = place(2)
+    both = both + place(1)
+    both = both + place(3)
+
     wait_bytes(lr_all, ZS - 1, lrz_send)
     wait_bytes(lr_all, ZS * (XS - 1), lrx_send)
 
     @pl.when(self_adapter)
     def _():
-        wait_bytes(adapter_send, 1, own_sem.at[1])
+        wait_bytes(adapter_send, 1, own_sem)
         wait_bytes(adapter_send, 7, ad_send)
         wait_bytes(adapter_recv, 7, ad_recv)
 
@@ -223,76 +241,53 @@
         wait_bytes(adapter_send, 8, ad_send)
         wait_bytes(adapter_recv, 8, ad_recv)
 
-    wait_bytes(msg, MP - 1, send_sem)
-    wait_bytes(recv, MP - 1, recv_sem)
-
-
-def owner_kernel(
-    recv, up_hbm, adapter_recv, qg_in, key_out, value_out, lrg_out, aug_out, qg_out,
-    recv_v, grads, up, terms, qg_v, in_sem, out_sem, side_sem,
-):
-    parts = 4
-    heads = MP // parts
-    width = heads * HS
-    arrive = [
-        pltpu.make_async_copy(
-            recv.at[pl.ds(c * heads, heads)], recv_v.at[pl.ds(c * heads, heads)], in_sem.at[c]
-        )
-        for c in range(parts)
-    ]
-    side = [
-        pltpu.make_async_copy(a, b, side_sem.at[i])
-        for i, (a, b) in enumerate(((up_hbm, up), (adapter_recv, terms), (qg_in, qg_v)))
-    ]
-    for copy in arrive + side:
-        copy.start()
-    leave = []
-    for c in range(parts):
-        arrive[c].wait()
-        for j in range(c * heads // 2, (c + 1) * heads // 2):
-            a = recv_v[2 * j]
-            b = recv_v[2 * j + 1]
-            cols = slice(128 * j, 128 * j + 128)
-            grads[0:OWN, cols] = jnp.concatenate([a[:, :HS], b[:, :HS]], axis=1)
-            grads[OWN : 2 * OWN, cols] = jnp.concatenate([a[:, HS:], b[:, HS:]], axis=1)
-        cols = pl.ds(c * width, width)
-        for i, out in enumerate((key_out, value_out)):
-            copy = pltpu.make_async_copy(
-                grads.at[pl.ds(i * OWN, OWN), cols], out.at[:, cols], out_sem.at[2 * c + i]
-            )
-            copy.start()
-            leave.append(copy)
-    for copy in side:
-        copy.wait()
-    back = pltpu.make_async_copy(qg_v, qg_out, side_sem.at[3])
-    back.start()
-    total = ADAPTER_FACTOR * jnp.sum(terms[...], axis=0)
+    total = ADAPTER_FACTOR * jnp.sum(adapter_recv[...], axis=0)
     for r in range(8):
         aug_out[r : r + 1, :] = total[r // 4 : r // 4 + 1, r % 4 * RANK2 : (r % 4 + 1) * RANK2]
-    both = lax.dot_general(grads[...], up[...], NT, preferred_element_type=F32)
+
+    wait_bytes(msg, MP - 1, send_sem)
+    both = both + place(0)
     lane = lax.broadcasted_iota(jnp.int32, (OWN, RANK2), 1)
     lrg_out[...] = ADAPTER_FACTOR * jnp.where(lane < RANK2 // 2, both[:OWN], both[OWN:])
-    for copy in leave:
+
+
+def leave_kernel(grads, lrg, aug, qg, key_out, value_out, lrg_out, aug_out, qg_out, sem):
+    copies = [
+        pltpu.make_async_copy(a, b, sem.at[i])
+        for i, (a, b) in enumerate(
+            (
+                (grads.at[0:OWN], key_out),
+                (grads.at[OWN : 2 * OWN], value_out),
+                (lrg, lrg_out),
+                (aug, aug_out),
+                (qg, qg_out),
+            )
+        )
+    ]
+    for copy in copies:
+        copy.start()
+    for copy in copies:
         copy.wait()
-    back.wait()
 
 
 def local(query, kv_cache, out_grad, source_lengths, target_lengths, low_rank, adapter_up_matrix):
     any_spec = pl.BlockSpec(memory_space=pl.ANY)
     smem = pl.BlockSpec(memory_space=pltpu.SMEM)
     vmem = pl.BlockSpec(memory_space=pltpu.VMEM)
-    recv, adapter_recv, qg = pl.pallas_call(
+    inside = pl.pallas_call(
         exchange_kernel,
         out_shape=(
-            jax.ShapeDtypeStruct((MP, OWN, 2 * HS), BF16),
-            jax.ShapeDtypeStruct((DP, 2, 4 * RANK2), F32),
-            jax.ShapeDtypeStruct((HS, TQ), BF16),
+            pltpu.VMEM((2 * OWN, MP * HS), BF16),
+            pltpu.VMEM((OWN, RANK2), F32),
+            pltpu.VMEM((8, RANK2), F32),
+            pltpu.VMEM((HS, TQ), BF16),
         ),
-        in_specs=[any_spec, any_spec, any_spec, smem, smem, any_spec],
-        out_specs=(any_spec, any_spec, vmem),
+        in_specs=[any_spec, any_spec, any_spec, smem, smem, any_spec, any_spec],
+        out_specs=(vmem,) * 4,
         scratch_shapes=[
             pltpu.VMEM((S, 2 * HS), BF16),
             pltpu.VMEM((OWN, RANK2), BF16),
+            pltpu.VMEM((RANK2, MP * HS), BF16),
             pltpu.VMEM((2 * HS, 2 * TQ), BF16),
             pltpu.VMEM((S, TQ), F32),
             pltpu.VMEM((S, TQ), F32),
@@ -302,24 +297,27 @@
             pltpu.VMEM((MP, OWN, 4 * RANK2), F32),
             pltpu.VMEM((HS, 4 * RANK2), F32),
             pltpu.VMEM((8, 2, 4 * RANK2), F32),
-            pltpu.SemaphoreType.DMA((4,)),
-            pltpu.SemaphoreType.DMA,
-            pltpu.SemaphoreType.DMA,
-            pltpu.SemaphoreType.DMA,
-            pltpu.SemaphoreType.DMA,
-            pltpu.SemaphoreType.DMA,
-            pltpu.SemaphoreType.DMA,
-            pltpu.SemaphoreType.DMA,
-            pltpu.SemaphoreType.DMA,
-            pltpu.SemaphoreType.DMA((2,)),
+            pltpu.VMEM((MP, OWN, 2 * HS), BF16),
+            pltpu.VMEM((DP, 2, 4 * RANK2), F32),
+            pltpu.SemaphoreType.DMA((5,)),
+            pltpu.SemaphoreType.DMA,
+            pltpu.SemaphoreType.DMA((XS,)),
+            pltpu.SemaphoreType.DMA,
+            pltpu.SemaphoreType.DMA,
+            pltpu.SemaphoreType.DMA,
+            pltpu.SemaphoreType.DMA,
+            pltpu.SemaphoreType.DMA,
+            pltpu.SemaphoreType.DMA,
+            pltpu.SemaphoreType.DMA,
         ],
         compiler_params=pltpu.CompilerParams(
             collective_id=0, has_side_effects=True, vmem_limit_bytes=VMEM_LIMIT
         ),
         name="exchange",
-    )(query.T, kv_cache, out_grad.T, source_lengths, target_lengths, low_rank)
+    )(query.T, kv_cache, out_grad.T, source_lengths, target_lengths, low_rank, adapter_up_matrix)
+    inside = [pltpu.with_memory_space_constraint(a, pltpu.VMEM) for a in inside]
     key_gradient, value_grad, low_rank_gradient, adapter_up_gradient, query_grad = pl.pallas_call(
-        owner_kernel,
+        leave_kernel,
         out_shape=(
             jax.ShapeDtypeStruct((OWN, MP * HS), BF16),
             jax.ShapeDtypeStruct((OWN, MP * HS), BF16),
@@ -327,21 +325,12 @@
             jax.ShapeDtypeStruct((8, RANK2), F32),
             jax.ShapeDtypeStruct((HS, TQ), BF16),
         ),
-        in_specs=[any_spec] * 4,
-        out_specs=(any_spec, any_spec, vmem, vmem, any_spec),
-        scratch_shapes=[
-            pltpu.VMEM((MP, OWN, 2 * HS), BF16),
-            pltpu.VMEM((2 * OWN, MP * HS), BF16),
-            pltpu.VMEM((RANK2, MP * HS), BF16),
-            pltpu.VMEM((DP, 2, 4 * RANK2), F32),
-            pltpu.VMEM((HS, TQ), BF16),
-            pltpu.SemaphoreType.DMA((4,)),
-            pltpu.SemaphoreType.DMA((8,)),
-            pltpu.SemaphoreType.DMA((4,)),
-        ],
-        compiler_params=pltpu.CompilerParams(vmem_limit_bytes=VMEM_LIMIT),
-        name="owner",
-    )(recv, adapter_up_matrix, adapter_recv, qg)
+        in_specs=[vmem] * 4,
+        out_specs=(any_spec,) * 5,
+        scratch_shapes=[pltpu.SemaphoreType.DMA((5,))],
+        compiler_params=pltpu.CompilerParams(vmem_limit_bytes=LEAVE_VMEM),
+        name="leave",
+    )(*inside)
     return query_grad.T, key_gradient, value_grad, low_rank_gradient, adapter_up_gradient
 
 

time: 49.6 us -> 47.1 us (0.950)
  Pallas kernels: 48.8 us -> 46.3 us
    pallas_call x2, Pallas kernels: 48.8 us -> 46.3 us  [the longest x1 45.5 us: local(): pl.pallas_call(exchange_kernel, out_shape=(pltpu.VMEM((2 * OWN, MP * HS),...]
where the time goes in v4:
time: 47.1 us; the launch traced here: 46.9 us
  Pallas kernels  46.3 us (98%)
  between operations  0.64 us (1%)
    pallas_call x1, Pallas kernels, local(): pl.pallas_call(exchange_kernel, out_shape=(pltpu.VMEM((2 * OWN, MP * HS),...  45.5 us

profile of v4, /device:TPU:1, one launch (start us, length us, event | category | flops | bytes accessed | tf_op | source)
XLA Modules:
  0.0 46.9 jit_solution(1666625806130630776)
XLA Ops:
  0.6 45.5 %exchange.1 = (bf16[64,4096]{1,0:T(8,128)(2,1)S(1)}, f32[32,32]{1,0:T(8,128)S(1)}, f32[8,32]{1,0:T(8,128)S(1)}, bf16[64,256]{1,0:T(8,128)(2,1)S(1)}) custom-call(bf16[64,256]{1,0:T(8,128)(2,1)} %bitcast.3, bf16[2048,128]{1,0:T(8,128)(2,1)} %kv_hbm.1, bf16[64,256]{1,0:T(8,128)(2,1)} %bitcast.4, s32[1,8]{1,0:T(1,128)} %slen.1, s32[1,8]{1,0:T(1,128)} %tlen.1, ...), custom_call_target="tpu_custom_call" | custom-call | tf_op jit(solution)/shard_map/exchange/pallas_call | solution.py:277
  46.1 0.8 %leave.1 = (bf16[32,4096]{1,0:T(8,128)(2,1)}, bf16[32,4096]{1,0:T(8,128)(2,1)}, f32[32,32]{1,0:T(8,128)}, f32[8,32]{1,0:T(8,128)}, bf16[64,256]{1,0:T(8,128)(2,1)}) custom-call(bf16[64,4096]{1,0:T(8,128)(2,1)S(1)} %get-tuple-element.14.grads, f32[32,32]{1,0:T(8,128)S(1)} %get-tuple-element.15.lrg, f32[8,32]{1,0:T(8,128)S(1)} %get-tuple-element.16.aug, ...), custom_call_target="tpu_custom_call" | custom-call | tf_op jit(solution)/shard_map/leave/pallas_call | solution.py:319

commit v5 on v4

--- a/solution.py
+++ b/solution.py
@@ -36,9 +36,9 @@
 
 
 def exchange_kernel(
-    q_hbm, kv_hbm, g_hbm, slen, tlen, lr_hbm, up_hbm,
+    q_hbm, kv_hbm, g_hbm, slen_hbm, tlen_hbm, lr_hbm, up_hbm,
     grads, lrg_out, aug_out, qg_out,
-    kv_v, lr_v, up, w1, expo_s, dprob_s, ds_s, msg, lr_all, lr_full, term_s, adapter_send, recv, adapter_recv,
+    slen, tlen, kv_v, lr_v, up, w1, expo_s, dprob_s, ds_s, msg, lr_all, lr_full, term_s, adapter_send, recv, adapter_recv,
     in_sem, send_sem, recv_sem, lrz_send, lrz_recv, lrx_send, lrx_recv, ad_send, ad_recv, own_sem,
 ):
     p = lax.axis_index("dp")
@@ -73,12 +73,16 @@
                 (kv_hbm, kv_v),
                 (lr_hbm, lr_v),
                 (up_hbm, up),
+                (slen_hbm, slen),
+                (tlen_hbm, tlen),
             )
         )
     ]
     for c in loads:
         c.start()
 
+    loads[5].wait()
+    loads[6].wait()
     col = lax.broadcasted_iota(jnp.int32, (8, TQ), 1)
     lo = jnp.zeros((8, TQ), jnp.int32)
     hi = jnp.zeros((8, TQ), jnp.int32)
@@ -272,7 +276,6 @@
 
 def local(query, kv_cache, out_grad, source_lengths, target_lengths, low_rank, adapter_up_matrix):
     any_spec = pl.BlockSpec(memory_space=pl.ANY)
-    smem = pl.BlockSpec(memory_space=pltpu.SMEM)
     vmem = pl.BlockSpec(memory_space=pltpu.VMEM)
     inside = pl.pallas_call(
         exchange_kernel,
@@ -282,9 +285,11 @@
             pltpu.VMEM((8, RANK2), F32),
             pltpu.VMEM((HS, TQ), BF16),
         ),
-        in_specs=[any_spec, any_spec, any_spec, smem, smem, any_spec, any_spec],
+        in_specs=[any_spec] * 7,
         out_specs=(vmem,) * 4,
         scratch_shapes=[
+            pltpu.SMEM((1, NDOC), jnp.int32),
+            pltpu.SMEM((1, NDOC), jnp.int32),
             pltpu.VMEM((S, 2 * HS), BF16),
             pltpu.VMEM((OWN, RANK2), BF16),
             pltpu.VMEM((RANK2, MP * HS), BF16),
@@ -299,7 +304,7 @@
             pltpu.VMEM((8, 2, 4 * RANK2), F32),
             pltpu.VMEM((MP, OWN, 2 * HS), BF16),
             pltpu.VMEM((DP, 2, 4 * RANK2), F32),
-            pltpu.SemaphoreType.DMA((5,)),
+            pltpu.SemaphoreType.DMA((7,)),
             pltpu.SemaphoreType.DMA,
             pltpu.SemaphoreType.DMA((XS,)),
             pltpu.SemaphoreType.DMA,

time: 47.1 us -> 46.4 us (0.985)
  Pallas kernels: 46.3 us -> 45.6 us
    pallas_call x1, Pallas kernels: 45.5 us -> 44.8 us  [local(): pl.pallas_call(exchange_kernel, out_shape=(pltpu.VMEM((2 * OWN, MP * HS),...]
where the time goes in v5:
time: 46.4 us; the launch traced here: 46.3 us
  Pallas kernels  45.6 us (98%)
  between operations  0.64 us (1%)
    pallas_call x1, Pallas kernels, local(): pl.pallas_call(exchange_kernel, out_shape=(pltpu.VMEM((2 * OWN, MP * HS),...  44.8 us

profile of v5, /device:TPU:1, one launch (start us, length us, event | category | flops | bytes accessed | tf_op | source)
XLA Modules:
  0.0 46.3 jit_solution(11835243792879550695)
XLA Ops:
  0.6 44.8 %exchange.1 = (bf16[64,4096]{1,0:T(8,128)(2,1)S(1)}, f32[32,32]{1,0:T(8,128)S(1)}, f32[8,32]{1,0:T(8,128)S(1)}, bf16[64,256]{1,0:T(8,128)(2,1)S(1)}) custom-call(bf16[64,256]{1,0:T(8,128)(2,1)} %bitcast.3, bf16[2048,128]{1,0:T(8,128)(2,1)} %kv_hbm.1, bf16[64,256]{1,0:T(8,128)(2,1)} %bitcast.4, s32[1,8]{1,0:T(1,128)} %slen_hbm.1, s32[1,8]{1,0:T(1,128)} %tlen_hbm.1, ...), custom_call_target="tpu_custom_call" | custom-call | tf_op jit(solution)/shard_map/exchange/pallas_call | solution.py:280
  45.4 0.8 %leave.1 = (bf16[32,4096]{1,0:T(8,128)(2,1)}, bf16[32,4096]{1,0:T(8,128)(2,1)}, f32[32,32]{1,0:T(8,128)}, f32[8,32]{1,0:T(8,128)}, bf16[64,256]{1,0:T(8,128)(2,1)}) custom-call(bf16[64,4096]{1,0:T(8,128)(2,1)S(1)} %get-tuple-element.14.grads, f32[32,32]{1,0:T(8,128)S(1)} %get-tuple-element.15.lrg, f32[8,32]{1,0:T(8,128)S(1)} %get-tuple-element.16.aug, ...), custom_call_target="tpu_custom_call" | custom-call | tf_op jit(solution)/shard_map/leave/pallas_call | solution.py:324

commit v6 on v5

--- a/solution.py
+++ b/solution.py
@@ -158,7 +158,7 @@
             ).start()
 
     recv[pl.ds(m, 1)] = msg[pl.ds(m, 1)]
-    send(0, 36)
+    send(0, 32)
 
     qg_out[...] = lax.dot_general(kv_v[...], ds_s[...], TN, preferred_element_type=F32)[:HS].astype(BF16)
 
@@ -173,7 +173,7 @@
             device_id=(p, peer_of(j, 0)), device_id_type=MESH,
         ).start()
 
-    send(36, 50)
+    send(32, 46)
 
     wait_bytes(lr_all, ZS * (XS - 1), lrx_recv)
     gathered = lr_all[...].astype(F32)
@@ -196,6 +196,8 @@
     for k in range(8):
         adapter_send[k] = full[2 * k : 2 * k + 2]
 
+    send(46, 54)
+
     for k in range(8):
         dst_mp = 8 * gb + k
         me = jnp.logical_and(p == ga, dst_mp == m)
@@ -211,7 +213,7 @@
         def _():
             pltpu.make_async_copy(adapter_send.at[k], adapter_recv.at[p], own_sem).start()
 
-    send(50, MP - 1)
+    send(54, MP - 1)
 
     loads[4].wait()
 

time: 46.4 us -> 46.6 us (level)
  no operation moved by 1% of the time
where the time goes in v6:
time: 46.6 us; the launch traced here: 46.5 us
  Pallas kernels  45.8 us (98%)
  between operations  0.64 us (1%)
    pallas_call x1, Pallas kernels, local(): pl.pallas_call(exchange_kernel, out_shape=(pltpu.VMEM((2 * OWN, MP * HS),...  45 us

profile of v6, /device:TPU:1, one launch (start us, length us, event | category | flops | bytes accessed | tf_op | source)
XLA Modules:
  0.0 46.5 jit_solution(16627017565367074963)
XLA Ops:
  0.6 45.0 %exchange.1 = (bf16[64,4096]{1,0:T(8,128)(2,1)S(1)}, f32[32,32]{1,0:T(8,128)S(1)}, f32[8,32]{1,0:T(8,128)S(1)}, bf16[64,256]{1,0:T(8,128)(2,1)S(1)}) custom-call(bf16[64,256]{1,0:T(8,128)(2,1)} %bitcast.3, bf16[2048,128]{1,0:T(8,128)(2,1)} %kv_hbm.1, bf16[64,256]{1,0:T(8,128)(2,1)} %bitcast.4, s32[1,8]{1,0:T(1,128)} %slen_hbm.1, s32[1,8]{1,0:T(1,128)} %tlen_hbm.1, ...), custom_call_target="tpu_custom_call" | custom-call | tf_op jit(solution)/shard_map/exchange/pallas_call | solution.py:282
  45.6 0.8 %leave.1 = (bf16[32,4096]{1,0:T(8,128)(2,1)}, bf16[32,4096]{1,0:T(8,128)(2,1)}, f32[32,32]{1,0:T(8,128)}, f32[8,32]{1,0:T(8,128)}, bf16[64,256]{1,0:T(8,128)(2,1)}) custom-call(bf16[64,4096]{1,0:T(8,128)(2,1)S(1)} %get-tuple-element.14.grads, f32[32,32]{1,0:T(8,128)S(1)} %get-tuple-element.15.lrg, f32[8,32]{1,0:T(8,128)S(1)} %get-tuple-element.16.aug, ...), custom_call_target="tpu_custom_call" | custom-call | tf_op jit(solution)/shard_map/leave/pallas_call | solution.py:326

commit v7 on v6

--- a/solution.py
+++ b/solution.py
@@ -38,7 +38,7 @@
 def exchange_kernel(
     q_hbm, kv_hbm, g_hbm, slen_hbm, tlen_hbm, lr_hbm, up_hbm,
     grads, lrg_out, aug_out, qg_out,
-    slen, tlen, kv_v, lr_v, up, w1, expo_s, dprob_s, ds_s, msg, lr_all, lr_full, term_s, adapter_send, recv, adapter_recv,
+    slen, tlen, kv_v, lr_v, up, w1, expo_s, dprob_s, ds_s, msg, msg_t, lr_all, lr_full, term_s, adapter_send, recv, adapter_recv,
     in_sem, send_sem, recv_sem, lrz_send, lrz_recv, lrx_send, lrx_recv, ad_send, ad_recv, own_sem,
 ):
     p = lax.axis_index("dp")
@@ -165,6 +165,8 @@
     def wait_bytes(ref, count, sem):
         pltpu.make_async_copy(ref.at[pl.ds(0, count)], ref.at[pl.ds(0, count)], sem).wait()
 
+    msg_t[...] = msg[...].reshape(S, 2 * HS).T
+
     wait_bytes(lr_all, ZS - 1, lrz_recv)
     mine = lr_all.at[pl.ds(pl.multiple_of(x * ZS, ZS), ZS)]
     for j in (2, 1, 3):
@@ -181,9 +183,8 @@
         lr_full[:, 8 * j : 8 * j + 8, :] = pltpu.roll(
             gathered.reshape(MP * 8, 4 * RANK2), (4 - j) % 4 * RANK2, axis=1
         ).reshape(MP, 8, 4 * RANK2)
-    terms = lax.dot_general(
-        msg[...].reshape(S, 2 * HS), lr_full[...].reshape(S, 4 * RANK2).astype(BF16), TN,
-        preferred_element_type=F32,
+    terms = jnp.dot(
+        msg_t[...], lr_full[...].reshape(S, 4 * RANK2).astype(BF16), preferred_element_type=F32
     )
     lane = lax.broadcasted_iota(jnp.int32, (HS, 4 * RANK2), 1)
     term_s[...] = jnp.where(lane < RANK2 // 2, terms[:HS], terms[HS:])
@@ -300,6 +301,7 @@
             pltpu.VMEM((S, TQ), F32),
             pltpu.VMEM((S, TQ), BF16),
             pltpu.VMEM((MP, OWN, 2 * HS), BF16),
+            pltpu.VMEM((2 * HS, S), BF16),
             pltpu.VMEM((MP, 8, 4 * RANK2), BF16),
             pltpu.VMEM((MP, OWN, 4 * RANK2), F32),
             pltpu.VMEM((HS, 4 * RANK2), F32),

time: 46.6 us -> 46.6 us (level)
  no operation moved by 1% of the time
where the time goes in v7:
time: 46.6 us; the launch traced here: 46.4 us
  Pallas kernels  45.8 us (98%)
  between operations  0.64 us (1%)
    pallas_call x1, Pallas kernels, local(): pl.pallas_call(exchange_kernel, out_shape=(pltpu.VMEM((2 * OWN, MP * HS),...  44.9 us

profile of v7, /device:TPU:1, one launch (start us, length us, event | category | flops | bytes accessed | tf_op | source)
XLA Modules:
  0.0 46.4 jit_solution(10863018731575283138)
XLA Ops:
  0.6 44.9 %exchange.1 = (bf16[64,4096]{1,0:T(8,128)(2,1)S(1)}, f32[32,32]{1,0:T(8,128)S(1)}, f32[8,32]{1,0:T(8,128)S(1)}, bf16[64,256]{1,0:T(8,128)(2,1)S(1)}) custom-call(bf16[64,256]{1,0:T(8,128)(2,1)} %bitcast.3, bf16[2048,128]{1,0:T(8,128)(2,1)} %kv_hbm.1, bf16[64,256]{1,0:T(8,128)(2,1)} %bitcast.4, s32[1,8]{1,0:T(1,128)} %slen_hbm.1, s32[1,8]{1,0:T(1,128)} %tlen_hbm.1, ...), custom_call_target="tpu_custom_call" | custom-call | tf_op jit(solution)/shard_map/exchange/pallas_call | solution.py:283
  45.6 0.8 %leave.1 = (bf16[32,4096]{1,0:T(8,128)(2,1)}, bf16[32,4096]{1,0:T(8,128)(2,1)}, f32[32,32]{1,0:T(8,128)}, f32[8,32]{1,0:T(8,128)}, bf16[64,256]{1,0:T(8,128)(2,1)}) custom-call(bf16[64,4096]{1,0:T(8,128)(2,1)S(1)} %get-tuple-element.14.grads, f32[32,32]{1,0:T(8,128)S(1)} %get-tuple-element.15.lrg, f32[8,32]{1,0:T(8,128)S(1)} %get-tuple-element.16.aug, ...), custom_call_target="tpu_custom_call" | custom-call | tf_op jit(solution)/shard_map/leave/pallas_call | solution.py:328
